TPU v7x, 32 devices: a whole 2x2x4 slice. The times are simulated.
32 devices in a mesh: turn: 8 (over z, y), col: 4 (over x, core).
Axes of the slice: x: 2, y: 2, z: 4, core: 2. Of those that a mesh axis runs over, the one named last changes fastest.
Arguments:
- right_sides: float32 [16, 256, 512], P('turn', 'col'), may hold values from -6 to 6
- fill_blocks: bfloat16 [16, 2, 256, 256], P('turn', None, None, 'col'), may hold values from -0.1875 to 0.1875
Outputs:
- reduced: float32 [16, 256, 512], P('turn', 'col')
All inputs are finite; a program needn't handle non-finite values.
Results may differ from a plain program's by a relative error of at most 0.0022.
Values may be sent and summed in bfloat16 or wider, within the bound.
A program may use at most 64 MiB of HBM per device.

v0:
```python
import jax
import jax.numpy as jnp
from jax import lax
from jax.sharding import PartitionSpec as P

LEVELS = 4


def shifted(array, axis, by):
    size = lax.axis_size(axis)
    pairs = [(i, i + by) for i in range(size) if 0 <= i + by < size]
    return lax.ppermute(array, axis, pairs)


def route(to_left, to_right, level_num):
    offset = 1 if level_num == 0 else 2 ** (level_num - 1)
    right_in = shifted(to_right, "turn", offset)
    left_in = to_left if level_num == 0 else shifted(to_left, "turn", -offset)
    return (left_in, right_in)


def shards(right_sides, fill_blocks):
    position = lax.axis_index("turn")
    kept_row = right_sides[0]
    odd_row = right_sides[1]
    for level_num in range(LEVELS):
        if level_num == 0:
            source_rhs = odd_row
            source_fill = fill_blocks[1]
            active = position >= 0
        else:
            distance = 2 ** (level_num - 1)
            source_rhs = kept_row
            source_fill = fill_blocks[0]
            active = position % (2 * distance) == distance
        rounded = source_rhs.astype(jnp.bfloat16)
        to_left = jnp.dot(source_fill[0], rounded, preferred_element_type=jnp.float32)
        to_right = jnp.dot(source_fill[1], rounded, preferred_element_type=jnp.float32)
        to_left = jnp.where(active, to_left, 0.0)
        to_right = jnp.where(active, to_right, 0.0)
        left_in, right_in = route(to_left, to_right, level_num)
        update = lax.psum_scatter(left_in + right_in, "col", scatter_dimension=0, tiled=True)
        kept_row = kept_row - update
    return jnp.stack([kept_row, odd_row])


def solution(mesh):
    placed = (P("turn", "col", None), P("turn", None, None, "col"))
    return jax.shard_map(
        shards, mesh=mesh, in_specs=placed, out_specs=P("turn", "col", None), check_vma=False
    )
```

profile of v0, /device:TPU:0, one launch (start us, length us, event | category | flops | bytes accessed | tf_op | source)
XLA Modules:
  0.0 202.7 jit_solution(4431797509987831601)
XLA Ops:
  6.5 0.0 reduce-scatter.5.cloned.1.call-start
  6.5 0.0 copy-start
  6.5 0.0 copy-start.1
  6.5 1.2 convolution_select_fusion.6
  7.8 4.9 %collective-permute-start = (f32[256,512]{1,0:T(8,128)S(1)}, f32[256,512]{1,0:T(8,128)S(1)}, u32[]{:S(2)}, u32[]{:S(2)}) collective-permute-start(f32[256,512]{1,0:T(8,128)S(1)} %convolution_select_fusion.6), channel_id=1, source_target_pairs={{0,4},{4,8},{8,12},{12,16},{16,20},{20,24},{24,28},{1,5},{5,9},{9,... | collective-permute-start | bytes 1572872 | tf_op jit(solution)/shard_map/ppermute | solution.py:12
  12.7 11.1 %collective-permute-done = f32[256,512]{1,0:T(8,128)S(1)} collective-permute-done((f32[256,512]{1,0:T(8,128)S(1)}, f32[256,512]{1,0:T(8,128)S(1)}, u32[]{:S(2)}, u32[]{:S(2)}) %collective-permute-start) | collective-permute-done | bytes 524320 | tf_op jit(solution)/shard_map/ppermute | solution.py:12
  23.8 0.0 copy-done
  23.8 0.0 copy-done.1
  23.8 1.1 fusion.6
  24.9 0.0 reduce-scatter.5.cloned.1.call-update
  24.9 0.0 reduce-scatter.7.cloned.1.call-start
  25.0 24.0 %reduce-scatter.5.cloned.1.call-done = f32[64,512]{1,0:T(8,128)} async-done(((f32[256,512]{1,0:T(8,128)}), f32[64,512]{1,0:T(8,128)}) %reduce-scatter.5.cloned.1.call-update) | async-done | bytes 131088 | tf_op jit(solution)/shard_map/reduce_scatter | solution.py:42
  48.9 0.9 fusion.10
  49.9 0.3 fusion.5
  50.1 0.3 fusion.4
  50.4 1.3 collective-permute-start.1
  51.7 4.6 %collective-permute-start.2 = (f32[256,512]{1,0:T(8,128)S(1)}, f32[256,512]{1,0:T(8,128)S(1)}, u32[]{:S(2)}, u32[]{:S(2)}) collective-permute-start(f32[256,512]{1,0:T(8,128)S(1)} %fusion.4), channel_id=1, source_target_pairs={{0,4},{4,8},{8,12},{12,16},{16,20},{20,24},{24,28},{1,5},{5,9},{9,... | collective-permute-start | bytes 1572872 | tf_op jit(solution)/shard_map/ppermute | solution.py:12
  56.3 9.5 %collective-permute-done.1 = f32[256,512]{1,0:T(8,128)S(1)} collective-permute-done((f32[256,512]{1,0:T(8,128)S(1)}, f32[256,512]{1,0:T(8,128)S(1)}, u32[]{:S(2)}, u32[]{:S(2)}) %collective-permute-start.1) | collective-permute-done | bytes 524320 | tf_op jit(solution)/shard_map/ppermute | solution.py:12
  65.8 11.1 %collective-permute-done.2 = f32[256,512]{1,0:T(8,128)S(1)} collective-permute-done((f32[256,512]{1,0:T(8,128)S(1)}, f32[256,512]{1,0:T(8,128)S(1)}, u32[]{:S(2)}, u32[]{:S(2)}) %collective-permute-start.2) | collective-permute-done | bytes 524320 | tf_op jit(solution)/shard_map/ppermute | solution.py:12
  76.9 0.9 add.32
  77.8 0.0 copy-start.2
  77.8 0.0 reduce-scatter.7.cloned.1.call-update
  77.8 0.0 reduce-scatter.9.cloned.1.call-start
  77.9 21.8 %reduce-scatter.7.cloned.1.call-done = f32[64,512]{1,0:T(8,128)} async-done(((f32[256,512]{1,0:T(8,128)}), f32[64,512]{1,0:T(8,128)}) %reduce-scatter.7.cloned.1.call-update) | async-done | bytes 131088 | tf_op jit(solution)/shard_map/reduce_scatter | solution.py:42
  99.7 0.0 copy-done.2
  99.7 0.9 fusion.9
  100.7 0.3 fusion.2
  100.9 0.3 fusion.3
  101.2 3.4 %collective-permute-start.4 = (f32[256,512]{1,0:T(8,128)S(1)}, f32[256,512]{1,0:T(8,128)S(1)}, u32[]{:S(2)}, u32[]{:S(2)}) collective-permute-start(f32[256,512]{1,0:T(8,128)S(1)} %fusion.2), channel_id=1, source_target_pairs={{0,8},{4,12},{8,16},{12,20},{16,24},{20,28},{1,9},{5,13},{9,17},{1... | collective-permute-start | bytes 1572872 | tf_op jit(solution)/shard_map/ppermute | solution.py:12
  104.7 1.3 collective-permute-start.3
  106.0 9.7 %collective-permute-done.4 = f32[256,512]{1,0:T(8,128)S(1)} collective-permute-done((f32[256,512]{1,0:T(8,128)S(1)}, f32[256,512]{1,0:T(8,128)S(1)}, u32[]{:S(2)}, u32[]{:S(2)}) %collective-permute-start.4) | collective-permute-done | bytes 524320 | tf_op jit(solution)/shard_map/ppermute | solution.py:12
  115.6 4.1 %collective-permute-done.3 = f32[256,512]{1,0:T(8,128)S(1)} collective-permute-done((f32[256,512]{1,0:T(8,128)S(1)}, f32[256,512]{1,0:T(8,128)S(1)}, u32[]{:S(2)}, u32[]{:S(2)}) %collective-permute-start.3) | collective-permute-done | bytes 524320 | tf_op jit(solution)/shard_map/ppermute | solution.py:12
  119.8 0.9 add.34
  120.6 0.0 reduce-scatter.9.cloned.1.call-update
  120.7 0.0 reduce-scatter.11.cloned.1.call-start
  120.7 20.8 %reduce-scatter.9.cloned.1.call-done = f32[64,512]{1,0:T(8,128)} async-done(((f32[256,512]{1,0:T(8,128)}), f32[64,512]{1,0:T(8,128)}) %reduce-scatter.9.cloned.1.call-update) | async-done | bytes 131088 | tf_op jit(solution)/shard_map/reduce_scatter | solution.py:42
  141.5 0.9 sub.14
  142.4 0.3 fusion
  142.7 0.3 fusion.1
  143.0 4.3 %collective-permute-start.6 = (f32[256,512]{1,0:T(8,128)S(1)}, f32[256,512]{1,0:T(8,128)S(1)}, u32[]{:S(2)}, u32[]{:S(2)}) collective-permute-start(f32[256,512]{1,0:T(8,128)S(1)} %fusion), channel_id=1, source_target_pairs={{0,16},{4,20},{8,24},{12,28},{1,17},{5,21},{9,25},{13,29},{2,18},{... | collective-permute-start | bytes 1572872 | tf_op jit(solution)/shard_map/ppermute | solution.py:12
  147.3 1.3 collective-permute-start.5
  148.6 9.7 %collective-permute-done.6 = f32[256,512]{1,0:T(8,128)S(1)} collective-permute-done((f32[256,512]{1,0:T(8,128)S(1)}, f32[256,512]{1,0:T(8,128)S(1)}, u32[]{:S(2)}, u32[]{:S(2)}) %collective-permute-start.6) | collective-permute-done | bytes 524320 | tf_op jit(solution)/shard_map/ppermute | solution.py:12
  158.4 16.2 %collective-permute-done.5 = f32[256,512]{1,0:T(8,128)S(1)} collective-permute-done((f32[256,512]{1,0:T(8,128)S(1)}, f32[256,512]{1,0:T(8,128)S(1)}, u32[]{:S(2)}, u32[]{:S(2)}) %collective-permute-start.5) | collective-permute-done | bytes 524320 | tf_op jit(solution)/shard_map/ppermute | solution.py:12
  174.6 0.9 add.36
  175.5 0.0 reduce-scatter.11.cloned.1.call-update
  175.5 0.0 slice-start
  175.5 19.0 %reduce-scatter.11.cloned.1.call-done = f32[64,512]{1,0:T(8,128)} async-done(((f32[256,512]{1,0:T(8,128)}), f32[64,512]{1,0:T(8,128)}) %reduce-scatter.11.cloned.1.call-update) | async-done | bytes 131088 | tf_op jit(solution)/shard_map/reduce_scatter | solution.py:42
  194.5 0.9 subtract_bitcast_fusion
  195.5 0.0 slice-done
  195.5 0.7 pad_maximum_fusion
Async XLA Ops:
  6.5 42.4 %reduce-scatter.5.cloned.1.call-start = ((), (), s32[]{:S(2)}) async-start(), calls=%async_computation.4 | async-start | bytes 655360 | tf_op jit(solution)/shard_map/reduce_scatter | solution.py:42
  6.5 17.3 %copy-start = (f32[2,64,512]{2,1,0:T(8,128)S(1)}, f32[2,64,512]{2,1,0:T(8,128)}, u32[]{:S(2)}) copy-start(f32[2,64,512]{2,1,0:T(8,128)} %param.2) | copy-start | bytes 786436
  6.5 17.3 %copy-start.1 = (bf16[2,2,256,64]{2,3,1,0:T(8,128)(2,1)S(1)}, bf16[2,2,256,64]{2,3,1,0:T(8,128)(2,1)}, u32[]{:S(2)}) copy-start(bf16[2,2,256,64]{2,3,1,0:T(8,128)(2,1)} %param.3) | copy-start | bytes 393220
  7.8 16.1 %collective-permute-start = (f32[256,512]{1,0:T(8,128)S(1)}, f32[256,512]{1,0:T(8,128)S(1)}, u32[]{:S(2)}, u32[]{:S(2)}) collective-permute-start(f32[256,512]{1,0:T(8,128)S(1)} %convolution_select_fusion.6), channel_id=1, source_target_pairs={{0,4},{4,8},{8,12},{12,16},{16,20},{20,24},{24,28},{1,5},{5,9},{9,... | collective-permute-start | bytes 1572872 | tf_op jit(solution)/shard_map/ppermute | solution.py:12
  24.9 74.8 %reduce-scatter.7.cloned.1.call-start = ((), (), s32[]{:S(2)}) async-start(), calls=%async_computation.5 | async-start | bytes 655360 | tf_op jit(solution)/shard_map/reduce_scatter | solution.py:42
  50.4 15.4 %collective-permute-start.1 = (f32[256,512]{1,0:T(8,128)S(1)}, f32[256,512]{1,0:T(8,128)S(1)}, u32[]{:S(2)}, u32[]{:S(2)}) collective-permute-start(f32[256,512]{1,0:T(8,128)S(1)} %fusion.5), channel_id=1, source_target_pairs={{4,0},{8,4},{12,8},{16,12},{20,16},{24,20},{28,24},{5,1},{9,5},{13... | collective-permute-start | bytes 1572872 | tf_op jit(solution)/shard_map/ppermute | solution.py:12
  51.7 25.2 %collective-permute-start.2 = (f32[256,512]{1,0:T(8,128)S(1)}, f32[256,512]{1,0:T(8,128)S(1)}, u32[]{:S(2)}, u32[]{:S(2)}) collective-permute-start(f32[256,512]{1,0:T(8,128)S(1)} %fusion.4), channel_id=1, source_target_pairs={{0,4},{4,8},{8,12},{12,16},{16,20},{20,24},{24,28},{1,5},{5,9},{9,... | collective-permute-start | bytes 1572872 | tf_op jit(solution)/shard_map/ppermute | solution.py:12
  77.8 21.9 %copy-start.2 = (f32[64,512]{1,0:T(8,128)S(1)}, f32[64,512]{1,0:T(8,128)}, u32[]{:S(2)}) copy-start(f32[64,512]{1,0:T(8,128)} %reduce-scatter.5.cloned.1.call-done) | copy-start | bytes 393220
  77.8 63.7 %reduce-scatter.9.cloned.1.call-start = ((), (), s32[]{:S(2)}) async-start(), calls=%async_computation.6 | async-start | bytes 655360 | tf_op jit(solution)/shard_map/reduce_scatter | solution.py:42
  101.2 14.4 %collective-permute-start.4 = (f32[256,512]{1,0:T(8,128)S(1)}, f32[256,512]{1,0:T(8,128)S(1)}, u32[]{:S(2)}, u32[]{:S(2)}) collective-permute-start(f32[256,512]{1,0:T(8,128)S(1)} %fusion.2), channel_id=1, source_target_pairs={{0,8},{4,12},{8,16},{12,20},{16,24},{20,28},{1,9},{5,13},{9,17},{1... | collective-permute-start | bytes 1572872 | tf_op jit(solution)/shard_map/ppermute | solution.py:12
  104.7 15.1 %collective-permute-start.3 = (f32[256,512]{1,0:T(8,128)S(1)}, f32[256,512]{1,0:T(8,128)S(1)}, u32[]{:S(2)}, u32[]{:S(2)}) collective-permute-start(f32[256,512]{1,0:T(8,128)S(1)} %fusion.3), channel_id=1, source_target_pairs={{8,0},{12,4},{16,8},{20,12},{24,16},{28,20},{9,1},{13,5},{17,9},{2... | collective-permute-start | bytes 1572872 | tf_op jit(solution)/shard_map/ppermute | solution.py:12
  120.7 73.9 %reduce-scatter.11.cloned.1.call-start = ((), (), s32[]{:S(2)}) async-start(), calls=%async_computation.7 | async-start | bytes 655360 | tf_op jit(solution)/shard_map/reduce_scatter | solution.py:42
  143.0 15.4 %collective-permute-start.6 = (f32[256,512]{1,0:T(8,128)S(1)}, f32[256,512]{1,0:T(8,128)S(1)}, u32[]{:S(2)}, u32[]{:S(2)}) collective-permute-start(f32[256,512]{1,0:T(8,128)S(1)} %fusion), channel_id=1, source_target_pairs={{0,16},{4,20},{8,24},{12,28},{1,17},{5,21},{9,25},{13,29},{2,18},{... | collective-permute-start | bytes 1572872 | tf_op jit(solution)/shard_map/ppermute | solution.py:12
  147.3 27.3 %collective-permute-start.5 = (f32[256,512]{1,0:T(8,128)S(1)}, f32[256,512]{1,0:T(8,128)S(1)}, u32[]{:S(2)}, u32[]{:S(2)}) collective-permute-start(f32[256,512]{1,0:T(8,128)S(1)} %fusion.1), channel_id=1, source_target_pairs={{16,0},{20,4},{24,8},{28,12},{17,1},{21,5},{25,9},{29,13},{18,2},{... | collective-permute-start | bytes 1572872 | tf_op jit(solution)/shard_map/ppermute | solution.py:12
  175.5 20.0 %slice-start = ((f32[2,64,512]{2,1,0:T(8,128)}), f32[1,64,512]{2,1,0:T(8,128)S(1)}, s32[]{:S(2)}) async-start(f32[2,64,512]{2,1,0:T(8,128)} %param.2), calls=%async_computation.8 | async-start | bytes 262144 | tf_op jit(solution)/shard_map/slice | solution.py:25
Sparse Core Ops, SparseCore 0:
  25.0 23.8 reduce-scatter.4
  78.0 21.7 reduce-scatter.6
  120.8 20.6 reduce-scatter.8
  175.6 18.8 reduce-scatter.10
where the time goes:
time: 203 us
  waiting for transfers between devices  157 us (77%)
  starting transfers between devices  21.3 us (10%)
  between operations  13.3 us (7%)
  other arithmetic  7.07 us (3%)
  matrix products  3.87 us (2%)
    reduce_scatter x4, waiting for transfers between devices, shards(): lax.psum_scatter(left_in + right_in, 'col', scatter_dimension=0, tiled=True)  85.6 us
    ppermute x7, waiting for transfers between devices, shifted(): return lax.ppermute(array, axis, pairs)  71.5 us
    ppermute x7, starting transfers between devices, shifted(): return lax.ppermute(array, axis, pairs)  21.2 us
  transfers between devices with their start and end apart: 11, of which 11 were waited for; matrix products, arithmetic and copies ran while one was open for 0% of the time, Pallas kernels for 0%

commit v1 on v0

v1 whole, which is shorter than its diff:
```python
import functools

import jax
import jax.numpy as jnp
from jax import lax
from jax.experimental import pallas as pl
from jax.experimental.pallas import tpu as pltpu
from jax.sharding import PartitionSpec as P

LEVELS = 4
MESH = pl.DeviceIdType.MESH
F32 = jnp.float32
BF16 = jnp.bfloat16


def kernel(T, C, rs_ref, fill_ref, out_ref, pk, qs, q0, st, acc, cs0, cs, r0, rv, fin, ao,
           ph_s, ph_r, l0_s, l0_r, ch_s, ch_r, fi_s, fi_r, ao_s, ao_r):
    b, r = q0.shape[1], q0.shape[2]
    half = fill_ref.shape[3]
    p, c = lax.axis_index("turn"), lax.axis_index("col")
    last = LEVELS - 1

    def is_source(k):
        d = 2 ** (k - 1)
        return lax.rem(p, 2 * d) == d

    def is_kept(k):
        return lax.rem(p, 2 ** k) == 0

    def in_level(k):
        return lax.rem(p, 2 ** (k - 1)) == 0

    barrier = pltpu.get_barrier_semaphore()

    def greet(pt, pc):
        pl.semaphore_signal(barrier, inc=1, device_id=(pt, pc), device_id_type=MESH)

    peers = [lax.rem(c + off, C) for off in range(1, C)]
    for pc in peers:
        greet(p, pc)
    count = jnp.int32(C - 1)
    for k in range(1, LEVELS):
        d = 2 ** (k - 1)
        for there, pt in ((p >= d, p - d), (p + d < T, p + d)):
            cond = jnp.logical_and(in_level(k), there)

            @pl.when(cond)
            def _():
                greet(pt, c)
                if k == last:
                    for pc in peers:
                        greet(pt, pc)

            count = count + jnp.where(cond, C if k == last else 1, 0)

    par = lax.rem(c, 2)
    for l in (1, 0):
        pk[1 - l, c] = jnp.concatenate([fill_ref[l, par], fill_ref[l, 1 - par]], axis=-1)
        if l == 1:
            for i in range(C):
                qs[i] = rs_ref[1, :, i * r:(i + 1) * r].astype(BF16)
            q0[c] = qs[c]

    own = pl.ds(pl.multiple_of(c * r, r), r)
    st[c] = rs_ref[0, :, own]
    pl.semaphore_wait(barrier, count)

    def rcopy(src, dst, ss, rr, pt, pc):
        return pltpu.make_async_remote_copy(
            src_ref=src, dst_ref=dst, send_sem=ss, recv_sem=rr, device_id=(pt, pc), device_id_type=MESH)

    def phase(kind, off):
        pc = peers[off - 1]
        if kind == 0:
            src, dst = pk.at[0, c], pk.at[0, c]
        elif kind == 1:
            src, dst = qs.at[pc], q0.at[c]
        elif kind == 2:
            src, dst = rs_ref.at[0, :, pl.ds(pl.multiple_of(pc * r, r), r)], st.at[c]
        else:
            src, dst = pk.at[1, c], pk.at[1, c]
        return rcopy(src, dst, ph_s.at[kind, off - 1], ph_r.at[kind, off - 1], p, pc)

    offs = list(range(1, C))
    for kind in (0, 1, 2, 3):
        for off in offs:
            phase(kind, off).start()


    def fills(l):
        w = [pk[l, i] for i in range(C)]
        low = lax.broadcasted_iota(jnp.int32, w[0].shape, 1) < half
        left = jnp.concatenate([jnp.where(low, w[i], w[i + 1]) for i in range(0, C, 2)], axis=-1)
        right = jnp.concatenate([jnp.where(low, w[i + 1], w[i]) for i in range(0, C, 2)], axis=-1)
        return left, right

    def swap(q):
        return jnp.concatenate([q[(i ^ 1) * b:((i ^ 1) + 1) * b] for i in range(C)], axis=0)

    def dot(f, q):
        return jnp.dot(f, q, preferred_element_type=F32)

    for kind in (0, 1):
        for off in offs:
            phase(kind, off).wait_recv()
    left0, right0 = fills(0)
    q = jnp.concatenate([q0[i] for i in range(C)], axis=0)
    cs0[...] = dot(right0, swap(q))
    has_right, has_left = p + 1 < T, p >= 1
    send0 = rcopy(cs0, r0, l0_s, l0_r, p + 1, c)

    @pl.when(has_right)
    def _():
        send0.start()

    acc[...] = dot(left0, q)
    for kind in (2, 3):
        for off in offs:
            phase(kind, off).wait_recv()

    @pl.when(has_left)
    def _():
        rcopy(cs0, r0, l0_s, l0_r, p, c).wait_recv()
        acc[...] += r0[...]

    def piece(i):
        return pl.ds(pl.multiple_of(i * b, b), b)

    def out_copy(off):
        pc = peers[off - 1]
        return rcopy(acc.at[piece(pc)], ao.at[c], ao_s.at[off - 1], ao_r.at[off - 1], p, pc)

    def start_out():
        for off in offs:
            out_copy(off).start()
        ao[c] = acc[piece(c)]

    def chain_copy(k, side):
        d = 2 ** (k - 1)
        return rcopy(cs.at[side], rv.at[k - 1, side], ch_s.at[side], ch_r.at[k - 1, side],
                     p - d if side == 0 else p + d, c)

    def final_copy(side, i):
        d = 2 ** (last - 1)
        return rcopy(cs.at[side, piece(i)], fin.at[side, c], fi_s.at[side, i], fi_r.at[side, c],
                     p - d if side == 0 else p + d, i)

    def final_recv(side, i):
        return rcopy(cs.at[side, piece(0)], fin.at[side, i], fi_s.at[side, i], fi_r.at[side, i], p, i)

    for k in range(1, LEVELS):
        d = 2 ** (k - 1)

        @pl.when(is_source(k))
        def _():
            state = jnp.concatenate([st[i] for i in range(C)], axis=0) - acc[...]
            qk = state.astype(BF16)
            left1, right1 = fills(1)
            cs[0] = dot(left1, qk)
            if k == last:
                for i in range(C):
                    final_copy(0, i).start()
            else:
                chain_copy(k, 0).start()

            @pl.when(p + d < T)
            def _():
                cs[1] = dot(right1, swap(qk))
                if k == last:
                    for i in range(C):
                        final_copy(1, i).start()
                else:
                    chain_copy(k, 1).start()

            start_out()

        @pl.when(is_kept(k))
        def _():
            if k == last:
                start_out()
            else:
                @pl.when(p + d < T)
                def _():
                    chain_copy(k, 0).wait_recv()
                    acc[...] += rv[k - 1, 0]

                @pl.when(p >= d)
                def _():
                    chain_copy(k, 1).wait_recv()
                    acc[...] += rv[k - 1, 1]

    out_ref[1] = rs_ref[1]
    for off in offs:
        out_copy(off).wait_recv()
    for i in range(C):
        cols = slice(i * r, (i + 1) * r)
        out_ref[0, :, cols] = rs_ref[0, :, cols] - ao[i]
    D = 2 ** (last - 1)
    for side, there in ((0, p + D < T), (1, p >= D)):
        @pl.when(jnp.logical_and(is_kept(last), there))
        def _():
            for i in range(C):
                final_recv(side, i).wait_recv()
                cols = slice(i * r, (i + 1) * r)
                out_ref[0, :, cols] -= fin[side, i]

    for kind in range(4):
        for off in offs:
            phase(kind, off).wait_send()

    @pl.when(has_right)
    def _():
        send0.wait_send()

    for k in range(1, LEVELS):
        d = 2 ** (k - 1)
        for side, there in ((0, p >= d), (1, p + d < T)):
            @pl.when(jnp.logical_and(is_source(k), there))
            def _():
                if k == last:
                    for i in range(C):
                        final_copy(side, i).wait_send()
                else:
                    chain_copy(k, side).wait_send()
    for off in offs:
        out_copy(off).wait_send()


def shards(T, C, right_sides, fill_blocks):
    _, b, R = right_sides.shape
    B = fill_blocks.shape[2]
    r = R // C
    dma = pltpu.SemaphoreType.DMA
    vm = pl.BlockSpec(memory_space=pltpu.VMEM)
    return pl.pallas_call(
        functools.partial(kernel, T, C),
        out_shape=jax.ShapeDtypeStruct(right_sides.shape, F32),
        in_specs=[vm, vm],
        out_specs=vm,
        scratch_shapes=[
            pltpu.VMEM((2, C, B, 2 * fill_blocks.shape[3]), BF16),
            pltpu.VMEM((C, b, r), BF16),
            pltpu.VMEM((C, b, r), BF16),
            pltpu.VMEM((C, b, r), F32),
            pltpu.VMEM((B, r), F32),
            pltpu.VMEM((B, r), F32),
            pltpu.VMEM((2, B, r), F32),
            pltpu.VMEM((B, r), F32),
            pltpu.VMEM((LEVELS - 1, 2, B, r), F32),
            pltpu.VMEM((2, C, b, r), F32),
            pltpu.VMEM((C, b, r), F32),
            dma((4, C - 1)), dma((4, C - 1)),
            dma, dma,
            dma((2,)), dma((LEVELS - 1, 2)),
            dma((2, C)), dma((2, C)),
            dma((C - 1,)), dma((C - 1,)),
        ],
        compiler_params=pltpu.CompilerParams(collective_id=0, has_side_effects=True),
    )(right_sides, fill_blocks)


def solution(mesh):
    placed = (P("turn", "col", None), P("turn", None, None, "col"))
    return jax.shard_map(
        functools.partial(shards, mesh.shape["turn"], mesh.shape["col"]),
        mesh=mesh, in_specs=placed, out_specs=P("turn", "col", None), check_vma=False
    )
```

time: 203 us -> 38.1 us (0.19)
  waiting for transfers between devices: 157 us -> 0 us
  Pallas kernels: 0 us -> 34.5 us
  starting transfers between devices: 21.3 us -> 0 us
  between operations: 13.3 us -> 0.01 us
  other arithmetic: 7.07 us -> 0 us
  matrix products: 3.87 us -> 0 us
  local copies, waits for them, and re-layouts: 0.02 us -> 3.42 us
    reduce_scatter x4 -> x0, waiting for transfers between devices: 85.6 us -> none  [shards(): lax.psum_scatter(left_in + right_in, 'col', scatter_dimension=0, tiled=True)]
    ppermute x7 -> x0, waiting for transfers between devices: 71.5 us -> none  [shifted(): return lax.ppermute(array, axis, pairs)]
    pallas_call x0 -> x1, Pallas kernels: none -> 34.5 us  [shards(): pl.pallas_call(functools.partial(kernel, T, C), out_shape=jax.ShapeDtypeS...]
    ppermute x7 -> x0, starting transfers between devices: 21.2 us -> none  [shifted(): return lax.ppermute(array, axis, pairs)]
    dot_general x8 -> x0, matrix products: 3.87 us -> none  [the longest x4 2.01 us: shards(): jnp.dot(source_fill[1], rounded, preferred_element_type=jnp.float32)]
    unnamed x6 -> x2, local copies, waits for them, and re-layouts: 0.01 us -> 3.42 us
    add x3 -> x0, other arithmetic: 2.64 us -> none  [shards(): left_in + right_in]
  transfers between devices with their start and end apart: 11 -> 0, of which waited for: 11 -> 0; matrix products, arithmetic and copies ran while one was open for 0% -> 0% of each run, Pallas kernels for 0% -> 0%
where the time goes in v1:
time: 38.1 us; the launch traced here: 37.9 us
  Pallas kernels  34.5 us (91%)
  local copies, waits for them, and re-layouts  3.42 us (9%)
    pallas_call x1, Pallas kernels, shards(): pl.pallas_call(functools.partial(kernel, T, C), out_shape=jax.ShapeDtypeS...  34.5 us
    unnamed x2, local copies, waits for them, and re-layouts  3.42 us

profile of v1, /device:TPU:0, one launch (start us, length us, event | category | flops | bytes accessed | tf_op | source)
XLA Modules:
  0.0 37.9 jit_solution(13316493762538576560)
XLA Ops:
  0.0 1.7 %copy.3.fill_ref = bf16[2,2,256,64]{3,2,1,0:T(8,128)(2,1)} copy(bf16[2,2,256,64]{2,3,1,0:T(8,128)(2,1)} %param.3) | data formatting | bytes 262144 | tf_op args[1]
  1.7 34.5 %shard_map.28 = f32[2,64,512]{2,1,0:T(8,128)} custom-call(f32[2,64,512]{2,1,0:T(8,128)} %rs_ref.1, bf16[2,2,256,64]{3,2,1,0:T(8,128)(2,1)} %copy.3.fill_ref), custom_call_target="tpu_custom_call" | custom-call | tf_op jit(solution)/shard_map/pallas_call | solution.py:235
  36.2 1.7 %copy.5 = f32[2,64,512]{2,1,0:T(8,128)} copy(f32[2,64,512]{2,1,0:T(8,128)} %shard_map.28) | data formatting | bytes 524288

commit v2 on v0

v2 whole, which is shorter than its diff:
```python
import functools

import jax
import jax.numpy as jnp
from jax import lax
from jax.experimental import pallas as pl
from jax.experimental.pallas import tpu as pltpu
from jax.sharding import PartitionSpec as P

LEVELS = 4
MESH = pl.DeviceIdType.MESH
F32 = jnp.float32
BF16 = jnp.bfloat16


def kernel(T, C, rs_ref, fill_ref, out_ref, g0, qs, q0, st, acc, g, tf, tl, qb, qv, cs, fin, ao,
           ab_s, ab_r, cd_s, cd_r, st_s, st_r, fp_s, fp_r, fw_s, fw_r, ch_s, ch_r, fi_s, fi_r, ao_s, ao_r):
    b, r = st.shape[1], st.shape[2]
    p, c = lax.axis_index("turn"), lax.axis_index("col")
    last = LEVELS - 1
    offs = list(range(1, C))
    peers = [None] + [lax.rem(c + off, C) for off in offs]

    def is_source(k):
        d = 2 ** (k - 1)
        return lax.rem(p, 2 * d) == d

    def is_kept(k):
        return lax.rem(p, 2 ** k) == 0

    def in_level(k):
        return lax.rem(p, 2 ** (k - 1)) == 0

    def to(k, side):
        d = 2 ** (k - 1)
        return p - d if side == 0 else p + d

    def target(k, side):
        d = 2 ** (k - 1)
        return p >= d if side == 0 else p + d < T

    def sends(k, side):
        return jnp.logical_and(is_source(k), target(k, side))

    def receives(k, side):
        return jnp.logical_and(is_kept(k), target(k, 1 - side))

    barrier = pltpu.get_barrier_semaphore()

    def greet(pt, pc):
        pl.semaphore_signal(barrier, inc=1, device_id=(pt, pc), device_id_type=MESH)

    for off in offs:
        greet(p, peers[off])
    count = jnp.int32(C - 1)
    for k in range(1, LEVELS):
        wide = k == 1 or k == last
        for side in range(2):
            cond = jnp.logical_and(in_level(k), target(k, side))

            @pl.when(cond)
            def _():
                greet(to(k, side), c)
                if wide:
                    for off in offs:
                        greet(to(k, side), peers[off])

            count = count + jnp.where(cond, C if wide else 1, 0)

    for i in range(C):
        qs[i] = rs_ref[1, :, i * r:(i + 1) * r].astype(BF16)
    q0[0, c] = qs[c]
    g0[0, c] = fill_ref[1, 0]

    def columns(i):
        return pl.ds(pl.multiple_of(i * r, r), r)

    def piece(i):
        return pl.ds(pl.multiple_of(i * b, b), b)

    st[c] = rs_ref[0, :, columns(c)]
    for side in range(2):
        @pl.when(sends(last, side))
        def _():
            g[last - 1, side, c] = fill_ref[0, side]

    pl.semaphore_wait(barrier, count)

    def rcopy(src, dst, ss, rr, pt, pc):
        return pltpu.make_async_remote_copy(
            src_ref=src, dst_ref=dst, send_sem=ss, recv_sem=rr, device_id=(pt, pc), device_id_type=MESH)

    def own_fill(off):
        return rcopy(fill_ref.at[1, 0], g0.at[0, c], ab_s.at[0, off - 1], ab_r.at[0, off - 1], p, peers[off])

    def own_q(off):
        return rcopy(qs.at[peers[off]], q0.at[0, c], ab_s.at[1, off - 1], ab_r.at[1, off - 1], p, peers[off])

    def next_fill(off):
        pc = c if off == 0 else peers[off]
        return rcopy(fill_ref.at[1, 1], g0.at[1, c], cd_s.at[0, off], cd_r.at[0, off], p + 1, pc)

    def next_q(off):
        pc = c if off == 0 else peers[off]
        return rcopy(qs.at[pc], q0.at[1, c], cd_s.at[1, off], cd_r.at[1, off], p + 1, pc)

    def state_copy(off):
        return rcopy(rs_ref.at[0, :, columns(peers[off])], st.at[c], st_s.at[off - 1], st_r.at[off - 1], p, peers[off])

    def fill_piece(k, side):
        return rcopy(fill_ref.at[0, side], g.at[k - 1, side, c], fp_s.at[side], fp_r.at[k - 1, side], to(k, side), c)

    def forward(k, side, off):
        return rcopy(g.at[k - 1, side, c], g.at[k - 1, side, c],
                     fw_s.at[k - 1, side, off - 1], fw_r.at[k - 1, side, off - 1], p, peers[off])

    later = lax.rem(p, 2 ** last) > 0
    has_right, has_left = p + 1 < T, p >= 1

    @pl.when(has_right)
    def _():
        for off in offs + [0]:
            next_fill(off).start()
            next_q(off).start()

    for off in offs:
        own_fill(off).start()
        own_q(off).start()
    for k in range(1, last):
        for side in (1, 0):
            @pl.when(sends(k, side))
            def _():
                fill_piece(k, side).start()

    @pl.when(later)
    def _():
        for off in offs:
            state_copy(off).start()

    for k in range(1, last):
        for side in range(2):
            @pl.when(receives(k, side))
            def _():
                fill_piece(k, side).wait_recv()
                for off in offs:
                    forward(k, side, off).start()

    for side in range(2):
        @pl.when(sends(last, side))
        def _():
            for off in offs:
                forward(last, side, off).start()

    def whole(ref):
        return jnp.concatenate([ref[i] for i in range(C)], axis=0)

    def dot(f, q):
        return jnp.dot(f, q, preferred_element_type=F32)

    for off in offs:
        own_fill(off).wait_recv()
        own_q(off).wait_recv()
    acc[...] = dot(whole(g0.at[0]).T, whole(q0.at[0]))

    @pl.when(has_left)
    def _():
        for off in [0] + offs:
            next_fill(off).wait_recv()
            next_q(off).wait_recv()
        acc[...] += dot(whole(g0.at[1]).T, whole(q0.at[1]))

    def out_copy(off):
        return rcopy(acc.at[piece(peers[off])], ao.at[c], ao_s.at[off - 1], ao_r.at[off - 1], p, peers[off])

    def start_out():
        for off in offs:
            out_copy(off).start()
        ao[c] = acc[piece(c)]

    def chain_copy(k, side):
        return rcopy(qb, qv.at[k - 1, side], ch_s.at[side], ch_r.at[k - 1, side], to(k, side), c)

    def final_copy(side, i):
        return rcopy(cs.at[side, piece(i)], fin.at[side, c], fi_s.at[side, i], fi_r.at[side, c], to(last, side), i)

    def final_recv(side, i):
        return rcopy(cs.at[side, piece(0)], fin.at[side, i], fi_s.at[side, i], fi_r.at[side, i], p, i)

    @pl.when(later)
    def _():
        for off in offs:
            state_copy(off).wait_recv()

    for k in range(1, LEVELS):
        if k == last - 1:
            for side in range(2):
                @pl.when(sends(last, side))
                def _():
                    for off in offs:
                        forward(last, side, off).wait_recv()
                    tl[side] = whole(g.at[last - 1, side]).T

        if k < last:
            for side in range(2):
                @pl.when(receives(k, side))
                def _():
                    for off in offs:
                        forward(k, side, off).wait_recv()
                    tf[side] = whole(g.at[k - 1, side]).T

        @pl.when(is_source(k))
        def _():
            qk = (whole(st) - acc[...]).astype(BF16)
            if k < last:
                qb[...] = qk
            for side in (1, 0):
                @pl.when(target(k, side))
                def _():
                    if k == last:
                        cs[side] = dot(tl[side], qk)
                        for i in range(C):
                            final_copy(side, i).start()
                    else:
                        chain_copy(k, side).start()

            start_out()

        if k < last:
            for side in range(2):
                @pl.when(receives(k, side))
                def _():
                    chain_copy(k, side).wait_recv()
                    acc[...] += dot(tf[side], qv[k - 1, side])
        else:
            @pl.when(is_kept(k))
            def _():
                start_out()

    for off in offs:
        out_copy(off).wait_recv()
    for i in range(C):
        out_ref[:, i * r:(i + 1) * r] = ao[i]
    for side in range(2):
        @pl.when(receives(last, side))
        def _():
            for i in range(C):
                final_recv(side, i).wait_recv()
                out_ref[:, i * r:(i + 1) * r] += fin[side, i]

    for off in offs:
        own_fill(off).wait_send()
        own_q(off).wait_send()
        out_copy(off).wait_send()

    @pl.when(has_right)
    def _():
        for off in [0] + offs:
            next_fill(off).wait_send()
            next_q(off).wait_send()

    @pl.when(later)
    def _():
        for off in offs:
            state_copy(off).wait_send()

    for k in range(1, LEVELS):
        for side in range(2):
            @pl.when(sends(k, side))
            def _():
                if k == last:
                    for i in range(C):
                        final_copy(side, i).wait_send()
                    for off in offs:
                        forward(k, side, off).wait_send()
                else:
                    fill_piece(k, side).wait_send()
                    chain_copy(k, side).wait_send()

            if k < last:
                @pl.when(receives(k, side))
                def _():
                    for off in offs:
                        forward(k, side, off).wait_send()


def shards(T, C, right_sides, fill_blocks):
    _, b, R = right_sides.shape
    B = fill_blocks.shape[2]
    r = R // C
    n = fill_blocks.shape[3]
    dma = pltpu.SemaphoreType.DMA
    vm = pl.BlockSpec(memory_space=pltpu.VMEM)
    update = pl.pallas_call(
        functools.partial(kernel, T, C),
        out_shape=jax.ShapeDtypeStruct((b, R), F32),
        in_specs=[vm, vm],
        out_specs=vm,
        scratch_shapes=[
            pltpu.VMEM((2, C, n, B), BF16),
            pltpu.VMEM((C, b, r), BF16),
            pltpu.VMEM((2, C, b, r), BF16),
            pltpu.VMEM((C, b, r), F32),
            pltpu.VMEM((B, r), F32),
            pltpu.VMEM((LEVELS - 1, 2, C, n, B), BF16),
            pltpu.VMEM((2, B, B), BF16),
            pltpu.VMEM((2, B, B), BF16),
            pltpu.VMEM((B, r), BF16),
            pltpu.VMEM((LEVELS - 2, 2, B, r), BF16),
            pltpu.VMEM((2, B, r), F32),
            pltpu.VMEM((2, C, b, r), F32),
            pltpu.VMEM((C, b, r), F32),
            dma((2, C - 1)), dma((2, C - 1)),
            dma((2, C)), dma((2, C)),
            dma((C - 1,)), dma((C - 1,)),
            dma((2,)), dma((LEVELS - 2, 2)),
            dma((LEVELS - 1, 2, C - 1)), dma((LEVELS - 1, 2, C - 1)),
            dma((2,)), dma((LEVELS - 2, 2)),
            dma((2, C)), dma((2, C)),
            dma((C - 1,)), dma((C - 1,)),
        ],
        compiler_params=pltpu.CompilerParams(collective_id=0, has_side_effects=True),
    )(right_sides, jnp.swapaxes(fill_blocks, 2, 3))
    return right_sides - jnp.pad(update[None], ((0, 1), (0, 0), (0, 0)))


def solution(mesh):
    placed = (P("turn", "col", None), P("turn", None, None, "col"))
    return jax.shard_map(
        functools.partial(shards, mesh.shape["turn"], mesh.shape["col"]),
        mesh=mesh, in_specs=placed, out_specs=P("turn", "col", None), check_vma=False
    )
```

time: 203 us -> 31.1 us (0.15)
  waiting for transfers between devices: 157 us -> 0 us
  Pallas kernels: 0 us -> 29.3 us
  starting transfers between devices: 21.3 us -> 0 us
  between operations: 13.3 us -> 0.02 us
  other arithmetic: 7.07 us -> 1.63 us
  matrix products: 3.87 us -> 0 us
    reduce_scatter x4 -> x0, waiting for transfers between devices: 85.6 us -> none  [shards(): lax.psum_scatter(left_in + right_in, 'col', scatter_dimension=0, tiled=True)]
    ppermute x7 -> x0, waiting for transfers between devices: 71.5 us -> none  [shifted(): return lax.ppermute(array, axis, pairs)]
    pallas_call x0 -> x1, Pallas kernels: none -> 29.3 us  [shards(): pl.pallas_call(functools.partial(kernel, T, C), out_shape=jax.ShapeDtypeS...]
    ppermute x7 -> x0, starting transfers between devices: 21.2 us -> none  [shifted(): return lax.ppermute(array, axis, pairs)]
    dot_general x8 -> x0, matrix products: 3.87 us -> none  [the longest x4 2.01 us: shards(): jnp.dot(source_fill[1], rounded, preferred_element_type=jnp.float32)]
    add x3 -> x0, other arithmetic: 2.64 us -> none  [shards(): left_in + right_in]
  transfers between devices with their start and end apart: 11 -> 0, of which waited for: 11 -> 0; matrix products, arithmetic and copies ran while one was open for 0% -> 0% of each run, Pallas kernels for 0% -> 0%
where the time goes in v2:
time: 31.1 us; the launch traced here: 30.9 us
  Pallas kernels  29.3 us (94%)
  other arithmetic  1.63 us (5%)
    pallas_call x1, Pallas kernels, shards(): pl.pallas_call(functools.partial(kernel, T, C), out_shape=jax.ShapeDtypeS...  29.3 us
    sub x1, other arithmetic, shards(): return right_sides - jnp.pad(update[None], ((0, 1), (0, 0), (0, 0)))  1.63 us

profile of v2, /device:TPU:0, one launch (start us, length us, event | category | flops | bytes accessed | tf_op | source)
XLA Modules:
  0.0 30.9 jit_solution(3566206076108168316)
XLA Ops:
  0.0 0.0 copy-start
  0.0 29.3 %shard_map.28 = f32[64,512]{1,0:T(8,128)} custom-call(f32[2,64,512]{2,1,0:T(8,128)} %rs_ref.1, bf16[2,2,64,256]{3,2,1,0:T(8,128)(2,1)} %bitcast.3), custom_call_target="tpu_custom_call" | custom-call | tf_op jit(solution)/shard_map/pallas_call | solution.py:293
  29.3 0.0 copy-done
  29.3 1.6 %pad_subtract_fusion = f32[2,64,512]{2,1,0:T(8,128)} fusion(f32[2,64,512]{2,1,0:T(8,128)S(1)} %copy-done, f32[1,64,512]{2,1,0:T(8,128)} %bitcast.2), kind=kLoop, calls=%fused_computation | loop fusion | flops 65536 | bytes 655360 | tf_op jit(solution)/shard_map/sub | solution.py:323
Async XLA Ops:
  0.0 29.3 %copy-start = (f32[2,64,512]{2,1,0:T(8,128)S(1)}, f32[2,64,512]{2,1,0:T(8,128)}, u32[]{:S(2)}) copy-start(f32[2,64,512]{2,1,0:T(8,128)} %rs_ref.1) | copy-start | bytes 786436

commit v3 on v2

--- a/solution.py
+++ b/solution.py
@@ -20,6 +20,9 @@
     last = LEVELS - 1
     offs = list(range(1, C))
     peers = [None] + [lax.rem(c + off, C) for off in offs]
+    H = C // 2
+    partner = c + 1 - 2 * lax.rem(c, 2)
+    rest = [0] + list(range(H, C - 1))
 
     def is_source(k):
         d = 2 ** (k - 1)
@@ -90,15 +93,25 @@
         return pltpu.make_async_remote_copy(
             src_ref=src, dst_ref=dst, send_sem=ss, recv_sem=rr, device_id=(pt, pc), device_id_type=MESH)
 
-    def own_fill(off):
-        return rcopy(fill_ref.at[1, 0], g0.at[0, c], ab_s.at[0, off - 1], ab_r.at[0, off - 1], p, peers[off])
+    def passed(j):
+        return lax.rem(c - 2 * j + C, C)
+
+    def own_fill(i):
+        ss, rr = ab_s.at[0, i], ab_r.at[0, i]
+        if i < H:
+            return rcopy(fill_ref.at[1, 0], g0.at[0, c], ss, rr, p, peers[2 * i] if i else partner)
+        slot = g0.at[0, passed(i - H + 1)]
+        return rcopy(slot, slot, ss, rr, p, partner)
 
     def own_q(off):
         return rcopy(qs.at[peers[off]], q0.at[0, c], ab_s.at[1, off - 1], ab_r.at[1, off - 1], p, peers[off])
 
-    def next_fill(off):
-        pc = c if off == 0 else peers[off]
-        return rcopy(fill_ref.at[1, 1], g0.at[1, c], cd_s.at[0, off], cd_r.at[0, off], p + 1, pc)
+    def next_fill(i):
+        ss, rr = cd_s.at[0, i], cd_r.at[0, i]
+        if i < H:
+            return rcopy(fill_ref.at[1, 1], g0.at[1, c], ss, rr, p + 1, peers[2 * i] if i else c)
+        slot = g0.at[1, passed(i - H)]
+        return rcopy(slot, slot, ss, rr, p, partner)
 
     def next_q(off):
         pc = c if off == 0 else peers[off]
@@ -110,21 +123,33 @@
     def fill_piece(k, side):
         return rcopy(fill_ref.at[0, side], g.at[k - 1, side, c], fp_s.at[side], fp_r.at[k - 1, side], to(k, side), c)
 
-    def forward(k, side, off):
-        return rcopy(g.at[k - 1, side, c], g.at[k - 1, side, c],
-                     fw_s.at[k - 1, side, off - 1], fw_r.at[k - 1, side, off - 1], p, peers[off])
+    def forward(k, side, i):
+        slot = g.at[k - 1, side, c if i < H else passed(i - H + 1)]
+        pc = partner if i == 0 or i >= H else peers[2 * i]
+        return rcopy(slot, slot, fw_s.at[k - 1, side, i], fw_r.at[k - 1, side, i], p, pc)
+
+    def relay(copy):
+        for i in range(1, H):
+            copy(i).wait_recv()
+            copy(H + i - 1).start()
 
     later = lax.rem(p, 2 ** last) > 0
     has_right, has_left = p + 1 < T, p >= 1
 
     @pl.when(has_right)
     def _():
+        for i in reversed(range(H)):
+            next_fill(i).start()
+
+    for i in reversed(range(H)):
+        own_fill(i).start()
+
+    @pl.when(has_right)
+    def _():
         for off in offs + [0]:
-            next_fill(off).start()
             next_q(off).start()
 
     for off in offs:
-        own_fill(off).start()
         own_q(off).start()
     for k in range(1, last):
         for side in (1, 0):
@@ -142,14 +167,14 @@
             @pl.when(receives(k, side))
             def _():
                 fill_piece(k, side).wait_recv()
-                for off in offs:
-                    forward(k, side, off).start()
+                for i in reversed(range(H)):
+                    forward(k, side, i).start()
 
     for side in range(2):
         @pl.when(sends(last, side))
         def _():
-            for off in offs:
-                forward(last, side, off).start()
+            for i in reversed(range(H)):
+                forward(last, side, i).start()
 
     def whole(ref):
         return jnp.concatenate([ref[i] for i in range(C)], axis=0)
@@ -157,17 +182,33 @@
     def dot(f, q):
         return jnp.dot(f, q, preferred_element_type=F32)
 
-    for off in offs:
-        own_fill(off).wait_recv()
+    relay(own_fill)
+
+    @pl.when(has_left)
+    def _():
+        for i in range(H):
+            next_fill(i).wait_recv()
+            next_fill(H + i).start()
+
+    for i in rest:
+        own_fill(i).wait_recv()
+    for off in offs:
         own_q(off).wait_recv()
     acc[...] = dot(whole(g0.at[0]).T, whole(q0.at[0]))
 
     @pl.when(has_left)
     def _():
+        for i in range(H, C):
+            next_fill(i).wait_recv()
         for off in [0] + offs:
-            next_fill(off).wait_recv()
             next_q(off).wait_recv()
         acc[...] += dot(whole(g0.at[1]).T, whole(q0.at[1]))
+
+    for k in range(1, LEVELS):
+        for side in range(2):
+            @pl.when(receives(k, side) if k < last else sends(k, side))
+            def _():
+                relay(functools.partial(forward, k, side))
 
     def out_copy(off):
         return rcopy(acc.at[piece(peers[off])], ao.at[c], ao_s.at[off - 1], ao_r.at[off - 1], p, peers[off])
@@ -196,16 +237,16 @@
             for side in range(2):
                 @pl.when(sends(last, side))
                 def _():
-                    for off in offs:
-                        forward(last, side, off).wait_recv()
+                    for i in rest:
+                        forward(last, side, i).wait_recv()
                     tl[side] = whole(g.at[last - 1, side]).T
 
         if k < last:
             for side in range(2):
                 @pl.when(receives(k, side))
                 def _():
-                    for off in offs:
-                        forward(k, side, off).wait_recv()
+                    for i in rest:
+                        forward(k, side, i).wait_recv()
                     tf[side] = whole(g.at[k - 1, side]).T
 
         @pl.when(is_source(k))
@@ -247,16 +288,23 @@
                 final_recv(side, i).wait_recv()
                 out_ref[:, i * r:(i + 1) * r] += fin[side, i]
 
-    for off in offs:
-        own_fill(off).wait_send()
+    for i in range(C - 1):
+        own_fill(i).wait_send()
+    for off in offs:
         own_q(off).wait_send()
         out_copy(off).wait_send()
 
     @pl.when(has_right)
     def _():
+        for i in range(H):
+            next_fill(i).wait_send()
         for off in [0] + offs:
-            next_fill(off).wait_send()
             next_q(off).wait_send()
+
+    @pl.when(has_left)
+    def _():
+        for i in range(H, C):
+            next_fill(i).wait_send()
 
     @pl.when(later)
     def _():
@@ -270,8 +318,8 @@
                 if k == last:
                     for i in range(C):
                         final_copy(side, i).wait_send()
-                    for off in offs:
-                        forward(k, side, off).wait_send()
+                    for i in range(C - 1):
+                        forward(k, side, i).wait_send()
                 else:
                     fill_piece(k, side).wait_send()
                     chain_copy(k, side).wait_send()
@@ -279,8 +327,8 @@
             if k < last:
                 @pl.when(receives(k, side))
                 def _():
-                    for off in offs:
-                        forward(k, side, off).wait_send()
+                    for i in range(C - 1):
+                        forward(k, side, i).wait_send()
 
 
 def shards(T, C, right_sides, fill_blocks):

time: 31.1 us -> 28.5 us (0.916)
  Pallas kernels: 29.3 us -> 26.7 us
    pallas_call x1, Pallas kernels: 29.3 us -> 26.7 us  [shards(): pl.pallas_call(functools.partial(kernel, T, C), out_shape=jax.ShapeDtypeS...]
where the time goes in v3:
time: 28.5 us; the launch traced here: 28.4 us
  Pallas kernels  26.7 us (94%)
  other arithmetic  1.63 us (6%)
    pallas_call x1, Pallas kernels, shards(): pl.pallas_call(functools.partial(kernel, T, C), out_shape=jax.ShapeDtypeS...  26.7 us
    sub x1, other arithmetic, shards(): return right_sides - jnp.pad(update[None], ((0, 1), (0, 0), (0, 0)))  1.63 us

profile of v3, /device:TPU:0, one launch (start us, length us, event | category | flops | bytes accessed | tf_op | source)
XLA Modules:
  0.0 28.4 jit_solution(6203491009346472430)
XLA Ops:
  0.0 0.0 copy-start
  0.0 26.7 %shard_map.28 = f32[64,512]{1,0:T(8,128)} custom-call(f32[2,64,512]{2,1,0:T(8,128)} %rs_ref.1, bf16[2,2,64,256]{3,2,1,0:T(8,128)(2,1)} %bitcast.3), custom_call_target="tpu_custom_call" | custom-call | tf_op jit(solution)/shard_map/pallas_call | solution.py:341
  26.7 0.0 copy-done
  26.7 1.6 %pad_subtract_fusion = f32[2,64,512]{2,1,0:T(8,128)} fusion(f32[2,64,512]{2,1,0:T(8,128)S(1)} %copy-done, f32[1,64,512]{2,1,0:T(8,128)} %bitcast.2), kind=kLoop, calls=%fused_computation | loop fusion | flops 65536 | bytes 655360 | tf_op jit(solution)/shard_map/sub | solution.py:371
Async XLA Ops:
  0.0 26.7 %copy-start = (f32[2,64,512]{2,1,0:T(8,128)S(1)}, f32[2,64,512]{2,1,0:T(8,128)}, u32[]{:S(2)}) copy-start(f32[2,64,512]{2,1,0:T(8,128)} %rs_ref.1) | copy-start | bytes 786436

commit v4 on v3

--- a/solution.py
+++ b/solution.py
@@ -258,7 +258,7 @@
                 @pl.when(target(k, side))
                 def _():
                     if k == last:
-                        cs[side] = dot(tl[side], qk)
+                        cs[side] = dot(tl[side], qk).astype(BF16)
                         for i in range(C):
                             final_copy(side, i).start()
                     else:
@@ -286,7 +286,7 @@
         def _():
             for i in range(C):
                 final_recv(side, i).wait_recv()
-                out_ref[:, i * r:(i + 1) * r] += fin[side, i]
+                out_ref[:, i * r:(i + 1) * r] += fin[side, i].astype(F32)
 
     for i in range(C - 1):
         own_fill(i).wait_send()
@@ -354,8 +354,8 @@
             pltpu.VMEM((2, B, B), BF16),
             pltpu.VMEM((B, r), BF16),
             pltpu.VMEM((LEVELS - 2, 2, B, r), BF16),
-            pltpu.VMEM((2, B, r), F32),
-            pltpu.VMEM((2, C, b, r), F32),
+            pltpu.VMEM((2, B, r), BF16),
+            pltpu.VMEM((2, C, b, r), BF16),
             pltpu.VMEM((C, b, r), F32),
             dma((2, C - 1)), dma((2, C - 1)),
             dma((2, C)), dma((2, C)),

time: 28.5 us -> 28.1 us (0.986)
  Pallas kernels: 26.7 us -> 26.3 us
    pallas_call x1, Pallas kernels: 26.7 us -> 26.3 us  [shards(): pl.pallas_call(functools.partial(kernel, T, C), out_shape=jax.ShapeDtypeS...]
where the time goes in v4:
time: 28.1 us; the launch traced here: 28 us
  Pallas kernels  26.3 us (94%)
  other arithmetic  1.63 us (6%)
    pallas_call x1, Pallas kernels, shards(): pl.pallas_call(functools.partial(kernel, T, C), out_shape=jax.ShapeDtypeS...  26.3 us
    sub x1, other arithmetic, shards(): return right_sides - jnp.pad(update[None], ((0, 1), (0, 0), (0, 0)))  1.63 us

profile of v4, /device:TPU:0, one launch (start us, length us, event | category | flops | bytes accessed | tf_op | source)
XLA Modules:
  0.0 28.0 jit_solution(11045231306650250146)
XLA Ops:
  0.0 0.0 copy-start
  0.0 26.3 %shard_map.28 = f32[64,512]{1,0:T(8,128)} custom-call(f32[2,64,512]{2,1,0:T(8,128)} %rs_ref.1, bf16[2,2,64,256]{3,2,1,0:T(8,128)(2,1)} %bitcast.3), custom_call_target="tpu_custom_call" | custom-call | tf_op jit(solution)/shard_map/pallas_call | solution.py:341
  26.4 0.0 copy-done
  26.4 1.6 %pad_subtract_fusion = f32[2,64,512]{2,1,0:T(8,128)} fusion(f32[2,64,512]{2,1,0:T(8,128)S(1)} %copy-done, f32[1,64,512]{2,1,0:T(8,128)} %bitcast.2), kind=kLoop, calls=%fused_computation | loop fusion | flops 65536 | bytes 655360 | tf_op jit(solution)/shard_map/sub | solution.py:371
Async XLA Ops:
  0.0 26.4 %copy-start = (f32[2,64,512]{2,1,0:T(8,128)S(1)}, f32[2,64,512]{2,1,0:T(8,128)}, u32[]{:S(2)}) copy-start(f32[2,64,512]{2,1,0:T(8,128)} %rs_ref.1) | copy-start | bytes 786436

commit v5 on v3

--- a/solution.py
+++ b/solution.py
@@ -13,7 +13,7 @@
 BF16 = jnp.bfloat16
 
 
-def kernel(T, C, rs_ref, fill_ref, out_ref, g0, qs, q0, st, acc, g, tf, tl, qb, qv, cs, fin, ao,
+def kernel(T, C, rs_hbm, fill_hbm, out_ref, rs_ref, fill_ref, in_s, g0, qs, q0, st, acc, g, tf, tl, qb, qv, cs, fin, ao,
            ab_s, ab_r, cd_s, cd_r, st_s, st_r, fp_s, fp_r, fw_s, fw_r, ch_s, ch_r, fi_s, fi_r, ao_s, ao_r):
     b, r = st.shape[1], st.shape[2]
     p, c = lax.axis_index("turn"), lax.axis_index("col")
@@ -48,6 +48,12 @@
     def receives(k, side):
         return jnp.logical_and(is_kept(k), target(k, 1 - side))
 
+    loads = [pltpu.make_async_copy(rs_hbm.at[1], rs_ref.at[1], in_s.at[0]),
+             pltpu.make_async_copy(fill_hbm, fill_ref, in_s.at[1]),
+             pltpu.make_async_copy(rs_hbm.at[0], rs_ref.at[0], in_s.at[2])]
+    for load in loads:
+        load.start()
+
     barrier = pltpu.get_barrier_semaphore()
 
     def greet(pt, pc):
@@ -70,6 +76,8 @@
 
             count = count + jnp.where(cond, C if wide else 1, 0)
 
+    for load in loads:
+        load.wait()
     for i in range(C):
         qs[i] = rs_ref[1, :, i * r:(i + 1) * r].astype(BF16)
     q0[0, c] = qs[c]
@@ -341,9 +349,12 @@
     update = pl.pallas_call(
         functools.partial(kernel, T, C),
         out_shape=jax.ShapeDtypeStruct((b, R), F32),
-        in_specs=[vm, vm],
+        in_specs=[pl.BlockSpec(memory_space=pl.ANY)] * 2,
         out_specs=vm,
         scratch_shapes=[
+            pltpu.VMEM(right_sides.shape, F32),
+            pltpu.VMEM((2, 2, n, B), BF16),
+            dma((3,)),
             pltpu.VMEM((2, C, n, B), BF16),
             pltpu.VMEM((C, b, r), BF16),
             pltpu.VMEM((2, C, b, r), BF16),

time: 28.5 us -> 27.5 us (0.965)
  Pallas kernels: 26.7 us -> 25.7 us
    pallas_call x1, Pallas kernels: 26.7 us -> 25.7 us  [shards(): pl.pallas_call(functools.partial(kernel, T, C), out_shape=jax.ShapeDtypeS...]
where the time goes in v5:
time: 27.5 us; the launch traced here: 27.3 us
  Pallas kernels  25.7 us (93%)
  other arithmetic  1.63 us (6%)
    pallas_call x1, Pallas kernels, shards(): pl.pallas_call(functools.partial(kernel, T, C), out_shape=jax.ShapeDtypeS...  25.7 us
    sub x1, other arithmetic, shards(): return right_sides - jnp.pad(update[None], ((0, 1), (0, 0), (0, 0)))  1.63 us

profile of v5, /device:TPU:0, one launch (start us, length us, event | category | flops | bytes accessed | tf_op | source)
XLA Modules:
  0.0 27.3 jit_solution(16189608417454692767)
XLA Ops:
  0.0 0.0 copy-start
  0.0 25.7 %shard_map.28 = f32[64,512]{1,0:T(8,128)} custom-call(f32[2,64,512]{2,1,0:T(8,128)} %rs_hbm.1, bf16[2,2,64,256]{3,2,1,0:T(8,128)(2,1)} %bitcast.3), custom_call_target="tpu_custom_call" | custom-call | tf_op jit(solution)/shard_map/pallas_call | solution.py:349
  25.7 0.0 copy-done
  25.7 1.6 %pad_subtract_fusion = f32[2,64,512]{2,1,0:T(8,128)} fusion(f32[2,64,512]{2,1,0:T(8,128)S(1)} %copy-done, f32[1,64,512]{2,1,0:T(8,128)} %bitcast.2), kind=kLoop, calls=%fused_computation | loop fusion | flops 65536 | bytes 655360 | tf_op jit(solution)/shard_map/sub | solution.py:382
Async XLA Ops:
  0.0 25.7 %copy-start = (f32[2,64,512]{2,1,0:T(8,128)S(1)}, f32[2,64,512]{2,1,0:T(8,128)}, u32[]{:S(2)}) copy-start(f32[2,64,512]{2,1,0:T(8,128)} %rs_hbm.1) | copy-start | bytes 786436

commit v6 on v5

--- a/solution.py
+++ b/solution.py
@@ -144,31 +144,56 @@
     later = lax.rem(p, 2 ** last) > 0
     has_right, has_left = p + 1 < T, p >= 1
 
-    @pl.when(has_right)
-    def _():
+    def start_next_fill():
+        @pl.when(has_right)
+        def _():
+            for i in reversed(range(H)):
+                next_fill(i).start()
+
+    def start_next_q():
+        @pl.when(has_right)
+        def _():
+            for off in offs + [0]:
+                next_q(off).start()
+
+    def start_own_fill():
         for i in reversed(range(H)):
-            next_fill(i).start()
-
-    for i in reversed(range(H)):
-        own_fill(i).start()
-
-    @pl.when(has_right)
-    def _():
-        for off in offs + [0]:
-            next_q(off).start()
-
-    for off in offs:
-        own_q(off).start()
-    for k in range(1, last):
+            own_fill(i).start()
+
+    def start_own_q():
+        for off in offs:
+            own_q(off).start()
+
+    def start_state():
+        @pl.when(later)
+        def _():
+            for off in offs:
+                state_copy(off).start()
+
+    def start_pieces(k):
         for side in (1, 0):
             @pl.when(sends(k, side))
             def _():
                 fill_piece(k, side).start()
 
-    @pl.when(later)
-    def _():
-        for off in offs:
-            state_copy(off).start()
+    @pl.when(is_source(1))
+    def _():
+        start_own_fill()
+        start_own_q()
+        start_state()
+        start_pieces(1)
+        start_next_fill()
+        start_next_q()
+
+    @pl.when(is_kept(1))
+    def _():
+        start_next_fill()
+        start_own_fill()
+        start_next_q()
+        start_own_q()
+        for k in range(2, last):
+            start_pieces(k)
+        start_state()
 
     for k in range(1, last):
         for side in range(2):

time: 27.5 us -> 27.3 us (level)
  no operation moved by 1% of the time
where the time goes in v6:
time: 27.3 us; the launch traced here: 27.2 us
  Pallas kernels  25.5 us (93%)
  other arithmetic  1.63 us (6%)
    pallas_call x1, Pallas kernels, shards(): pl.pallas_call(functools.partial(kernel, T, C), out_shape=jax.ShapeDtypeS...  25.5 us
    sub x1, other arithmetic, shards(): return right_sides - jnp.pad(update[None], ((0, 1), (0, 0), (0, 0)))  1.63 us

profile of v6, /device:TPU:0, one launch (start us, length us, event | category | flops | bytes accessed | tf_op | source)
XLA Modules:
  0.0 27.2 jit_solution(12366964044423659090)
XLA Ops:
  0.0 0.0 copy-start
  0.0 25.5 %shard_map.28 = f32[64,512]{1,0:T(8,128)} custom-call(f32[2,64,512]{2,1,0:T(8,128)} %rs_hbm.1, bf16[2,2,64,256]{3,2,1,0:T(8,128)(2,1)} %bitcast.3), custom_call_target="tpu_custom_call" | custom-call | tf_op jit(solution)/shard_map/pallas_call | solution.py:374
  25.5 0.0 copy-done
  25.5 1.6 %pad_subtract_fusion = f32[2,64,512]{2,1,0:T(8,128)} fusion(f32[2,64,512]{2,1,0:T(8,128)S(1)} %copy-done, f32[1,64,512]{2,1,0:T(8,128)} %bitcast.2), kind=kLoop, calls=%fused_computation | loop fusion | flops 65536 | bytes 655360 | tf_op jit(solution)/shard_map/sub | solution.py:407
Async XLA Ops:
  0.0 25.5 %copy-start = (f32[2,64,512]{2,1,0:T(8,128)S(1)}, f32[2,64,512]{2,1,0:T(8,128)}, u32[]{:S(2)}) copy-start(f32[2,64,512]{2,1,0:T(8,128)} %rs_hbm.1) | copy-start | bytes 786436

commit v7 on v6

--- a/solution.py
+++ b/solution.py
@@ -251,8 +251,11 @@
             out_copy(off).start()
         ao[c] = acc[piece(c)]
 
-    def chain_copy(k, side):
-        return rcopy(qb, qv.at[k - 1, side], ch_s.at[side], ch_r.at[k - 1, side], to(k, side), c)
+    m = H * b
+
+    def chain_copy(k, side, h):
+        rows = pl.ds(h * m, m)
+        return rcopy(qb.at[rows], qv.at[k - 1, side, rows], ch_s.at[side, h], ch_r.at[k - 1, side, h], to(k, side), c)
 
     def final_copy(side, i):
         return rcopy(cs.at[side, piece(i)], fin.at[side, c], fi_s.at[side, i], fi_r.at[side, c], to(last, side), i)
@@ -284,27 +287,33 @@
 
         @pl.when(is_source(k))
         def _():
-            qk = (whole(st) - acc[...]).astype(BF16)
             if k < last:
-                qb[...] = qk
-            for side in (1, 0):
-                @pl.when(target(k, side))
-                def _():
-                    if k == last:
-                        cs[side] = dot(tl[side], qk)
-                        for i in range(C):
-                            final_copy(side, i).start()
-                    else:
-                        chain_copy(k, side).start()
+                for h in range(2):
+                    for i in range(h * H, (h + 1) * H):
+                        qb[i * b:(i + 1) * b] = (st[i] - acc[i * b:(i + 1) * b]).astype(BF16)
+                    for side in (1, 0):
+                        @pl.when(target(k, side))
+                        def _():
+                            chain_copy(k, side, h).start()
+            else:
+                qk = (whole(st) - acc[...]).astype(BF16)
+                for side in (1, 0):
+                    @pl.when(target(k, side))
+                    def _():
+                        for h in range(2):
+                            cs[side, h * m:(h + 1) * m] = dot(tl[side, h * m:(h + 1) * m], qk)
+                            for i in range(h * H, (h + 1) * H):
+                                final_copy(side, i).start()
 
             start_out()
 
         if k < last:
-            for side in range(2):
-                @pl.when(receives(k, side))
-                def _():
-                    chain_copy(k, side).wait_recv()
-                    acc[...] += dot(tf[side], qv[k - 1, side])
+            for h in range(2):
+                for side in range(2):
+                    @pl.when(receives(k, side))
+                    def _():
+                        chain_copy(k, side, h).wait_recv()
+                        acc[...] += dot(tf[side, :, h * m:(h + 1) * m], qv[k - 1, side, h * m:(h + 1) * m])
         else:
             @pl.when(is_kept(k))
             def _():
@@ -355,7 +364,8 @@
                         forward(k, side, i).wait_send()
                 else:
                     fill_piece(k, side).wait_send()
-                    chain_copy(k, side).wait_send()
+                    chain_copy(k, side, 0).wait_send()
+                    chain_copy(k, side, 1).wait_send()
 
             if k < last:
                 @pl.when(receives(k, side))
@@ -398,7 +408,7 @@
             dma((C - 1,)), dma((C - 1,)),
             dma((2,)), dma((LEVELS - 2, 2)),
             dma((LEVELS - 1, 2, C - 1)), dma((LEVELS - 1, 2, C - 1)),
-            dma((2,)), dma((LEVELS - 2, 2)),
+            dma((2, 2)), dma((LEVELS - 2, 2, 2)),
             dma((2, C)), dma((2, C)),
             dma((C - 1,)), dma((C - 1,)),
         ],

time: 27.3 us -> 27.6 us (1.011)
  Pallas kernels: 25.5 us -> 25.8 us
where the time goes in v7:
time: 27.6 us; the launch traced here: 27.4 us
  Pallas kernels  25.8 us (93%)
  other arithmetic  1.63 us (6%)
    pallas_call x1, Pallas kernels, shards(): pl.pallas_call(functools.partial(kernel, T, C), out_shape=jax.ShapeDtypeS...  25.8 us
    sub x1, other arithmetic, shards(): return right_sides - jnp.pad(update[None], ((0, 1), (0, 0), (0, 0)))  1.63 us

profile of v7, /device:TPU:0, one launch (start us, length us, event | category | flops | bytes accessed | tf_op | source)
XLA Modules:
  0.0 27.4 jit_solution(9349526787542619547)
XLA Ops:
  0.0 0.0 copy-start
  0.0 25.8 %shard_map.28 = f32[64,512]{1,0:T(8,128)} custom-call(f32[2,64,512]{2,1,0:T(8,128)} %rs_hbm.1, bf16[2,2,64,256]{3,2,1,0:T(8,128)(2,1)} %bitcast.3), custom_call_target="tpu_custom_call" | custom-call | tf_op jit(solution)/shard_map/pallas_call | solution.py:384
  25.8 0.0 copy-done
  25.8 1.6 %pad_subtract_fusion = f32[2,64,512]{2,1,0:T(8,128)} fusion(f32[2,64,512]{2,1,0:T(8,128)S(1)} %copy-done, f32[1,64,512]{2,1,0:T(8,128)} %bitcast.2), kind=kLoop, calls=%fused_computation | loop fusion | flops 65536 | bytes 655360 | tf_op jit(solution)/shard_map/sub | solution.py:417
Async XLA Ops:
  0.0 25.8 %copy-start = (f32[2,64,512]{2,1,0:T(8,128)S(1)}, f32[2,64,512]{2,1,0:T(8,128)}, u32[]{:S(2)}) copy-start(f32[2,64,512]{2,1,0:T(8,128)} %rs_hbm.1) | copy-start | bytes 786436

commit v8 on v5

--- a/solution.py
+++ b/solution.py
@@ -267,8 +267,10 @@
                 def _():
                     if k == last:
                         cs[side] = dot(tl[side], qk)
-                        for i in range(C):
-                            final_copy(side, i).start()
+                        for j in reversed(range(H)):
+                            to_col = peers[2 * j] if j else c
+                            final_copy(side, to_col).start()
+                            final_copy(side, to_col + 1 - 2 * lax.rem(to_col, 2)).start()
                     else:
                         chain_copy(k, side).start()
 

time: 27.5 us -> 27.7 us (level)
  no operation moved by 1% of the time
where the time goes in v8:
time: 27.7 us; the launch traced here: 27.6 us
  Pallas kernels  25.9 us (94%)
  other arithmetic  1.63 us (6%)
    pallas_call x1, Pallas kernels, shards(): pl.pallas_call(functools.partial(kernel, T, C), out_shape=jax.ShapeDtypeS...  25.9 us
    sub x1, other arithmetic, shards(): return right_sides - jnp.pad(update[None], ((0, 1), (0, 0), (0, 0)))  1.63 us

profile of v8, /device:TPU:0, one launch (start us, length us, event | category | flops | bytes accessed | tf_op | source)
XLA Modules:
  0.0 27.6 jit_solution(2145116257679104889)
XLA Ops:
  0.0 0.0 copy-start
  0.0 25.9 %shard_map.28 = f32[64,512]{1,0:T(8,128)} custom-call(f32[2,64,512]{2,1,0:T(8,128)} %rs_hbm.1, bf16[2,2,64,256]{3,2,1,0:T(8,128)(2,1)} %bitcast.3), custom_call_target="tpu_custom_call" | custom-call | tf_op jit(solution)/shard_map/pallas_call | solution.py:351
  25.9 0.0 copy-done
  25.9 1.6 %pad_subtract_fusion = f32[2,64,512]{2,1,0:T(8,128)} fusion(f32[2,64,512]{2,1,0:T(8,128)S(1)} %copy-done, f32[1,64,512]{2,1,0:T(8,128)} %bitcast.2), kind=kLoop, calls=%fused_computation | loop fusion | flops 65536 | bytes 655360 | tf_op jit(solution)/shard_map/sub | solution.py:384
Async XLA Ops:
  0.0 25.9 %copy-start = (f32[2,64,512]{2,1,0:T(8,128)S(1)}, f32[2,64,512]{2,1,0:T(8,128)}, u32[]{:S(2)}) copy-start(f32[2,64,512]{2,1,0:T(8,128)} %rs_hbm.1) | copy-start | bytes 786436
